TPU v7x, 256 devices: a whole 4x4x8 slice. The times are simulated.
256 devices in a mesh: dp: 4 (over x), expert: 64 (over y, z, core).
Axes of the slice: x: 4, y: 4, z: 8, core: 2. Of those that a mesh axis runs over, the one named last changes fastest.
Arguments:
- tokens: bfloat16 [8192, 4096], P('expert', 'dp'), may hold values from -6 to 6
- routes: int32 [8192, 4], P('expert'), may hold values from 0 to 63, all different within a row; in each aligned block of 128 rows (0 to 127, 128 to 255, ...) at most 16 rows name the same one
- route_weights: float32 [8192, 4], P('expert'), may hold values from 0.1 to 1
- gate_weight: bfloat16 [64, 4096, 1536], P('expert', None, 'dp'), may hold values from -0.09375 to 0.09375
- up_weight: bfloat16 [64, 4096, 1536], P('expert', None, 'dp'), may hold values from -0.09375 to 0.09375
- down_weight: bfloat16 [64, 1536, 4096], P('expert', 'dp'), may hold values from -0.15625 to 0.15625
- sketch_basis: bfloat16 [1536, 128], P('dp'), may hold values from -0.15625 to 0.15625
Outputs:
- mixed: bfloat16 [8192, 4096], P('expert', 'dp')
- sketch: float32 [64, 128, 1536], P('expert', None, 'dp')
Inputs may be any that keep to these rules, and one draw needn't show every extreme that they name: `routes`: each row names 4 different experts; within the rows of one device no expert is named more than 16 times, a bound that some block reaches.
All inputs are finite; a program needn't handle non-finite values.
Results may differ from a plain program's by a relative error of at most 0.017.
Values may be sent and summed in bfloat16 or wider, within the bound.
No kernel may reach another device: no remote copies, remote signals or barrier semaphores. Data moves between devices by JAX's collectives and lax.ppermute only.
A program may use at most 128 MiB of HBM per device.

v0:
```python
import jax
import jax.numpy as jnp
from jax import lax
from jax.sharding import PartitionSpec as P

ridge_term = 1.0


def gram_matrix(factor_rows):
    return jnp.dot(factor_rows.T, factor_rows, precision=lax.Precision.HIGHEST)


def body(tokens, routes, route_weights, gate_weight, up_weight, down_weight, sketch_basis):
    owners = lax.axis_size("expert")
    token_count, route_count = routes.shape
    pair_count = token_count * route_count
    capacity = 2 * pair_count // owners
    slot_total = owners * capacity
    route_list = routes.reshape(-1)
    onehot = (route_list[:, None] == jnp.arange(owners, dtype=jnp.int32)[None, :]).astype(jnp.int32)
    before = jnp.cumsum(onehot, axis=0) - onehot
    slot_of = jnp.sum(before * onehot, axis=1)
    counts = jnp.sum(onehot, axis=0)
    target = route_list * capacity + slot_of
    source_pair = (
        jnp.zeros((slot_total,), jnp.int32).at[target].set(jnp.arange(pair_count, dtype=jnp.int32))
    )
    source_token = source_pair // route_count
    count_wire = counts.astype(jnp.bfloat16)
    features = lax.all_gather(tokens, "dp", axis=1, tiled=True)
    outgoing = features[source_token].reshape(owners, capacity, features.shape[1])
    arrived, arrived_counts = (
        lax.all_to_all(outgoing, "expert", split_axis=0, concat_axis=0, tiled=True),
        lax.all_to_all(count_wire, "expert", split_axis=0, concat_axis=0, tiled=True),
    )
    width = arrived.shape[2]
    live_count = arrived_counts.astype(jnp.int32)
    live_mask = (jnp.arange(capacity, dtype=jnp.int32)[None, :] < live_count[:, None]).reshape(-1)
    slot_rows = jnp.where(
        live_mask[:, None], arrived.reshape(slot_total, width), jnp.zeros((), jnp.bfloat16)
    )
    gate_local = gate_weight[0]
    up_local = up_weight[0]
    down_local = down_weight[0]
    gate_val = jnp.dot(slot_rows, gate_local, preferred_element_type=jnp.float32)
    up_val = jnp.dot(slot_rows, up_local, preferred_element_type=jnp.float32)
    hidden_block = (jax.nn.silu(gate_val) * up_val).astype(jnp.bfloat16)
    partial_value = jnp.dot(hidden_block, down_local, preferred_element_type=jnp.float32)
    sums = lax.psum_scatter(
        partial_value.reshape(owners, capacity, width).astype(jnp.bfloat16),
        "dp",
        scatter_dimension=2,
        tiled=True,
    )
    returned = lax.all_to_all(sums, "expert", split_axis=0, concat_axis=0, tiled=True)
    picked = returned.reshape(slot_total, returned.shape[2])[target]
    weighted = jnp.einsum(
        "tkd,tk->td",
        picked.reshape(token_count, route_count, returned.shape[2]).astype(jnp.float32),
        route_weights,
    )
    mixed = weighted.astype(jnp.bfloat16)
    sketch_part = jnp.dot(hidden_block, sketch_basis, preferred_element_type=jnp.float32)
    sketch_width = sketch_part.shape[1]
    eye_matrix = jnp.eye(sketch_width, dtype=jnp.float32)
    sketch_full = lax.psum(sketch_part.astype(jnp.bfloat16), "dp").astype(jnp.float32)
    lower_factor = jnp.linalg.cholesky(gram_matrix(sketch_full) + ridge_term * eye_matrix)
    projected = jnp.dot(
        sketch_full.T, hidden_block.astype(jnp.float32), precision=lax.Precision.HIGHEST
    )
    whitened = jax.scipy.linalg.solve_triangular(lower_factor, projected, lower=True)
    return (mixed, whitened[None])


def solution(mesh):
    return jax.shard_map(
        body,
        mesh=mesh,
        in_specs=(
            P("expert", "dp"),
            P("expert", None),
            P("expert", None),
            P("expert", None, "dp"),
            P("expert", None, "dp"),
            P("expert", "dp", None),
            P("dp", None),
        ),
        out_specs=(P("expert", "dp"), P("expert", None, "dp")),
        check_vma=False,
    )
```

profile of v0, /device:TPU:8, one launch (start us, length us, event | category | flops | bytes accessed | tf_op | source)
XLA Modules:
  0.0 463.0 jit_solution(337429624355263726)
XLA Ops:
  9.1 1.2 reduce-window.6
  11.5 12.1 %all-to-all-start = ((bf16[64,1,1]{2,1,0:T(2,128)(2,1)}), bf16[64,1,1]{2,1,0:T(2,128)(2,1)S(1)}, u32[]{:S(2)}, u32[]{:S(2)}) async-start(bf16[64,1,1]{2,1,0:T(2,128)(2,1)} %copy.22), calls=%async_computation | async-start | bytes 65536 | tf_op jit(solution)/shard_map/all_to_all | solution.py:34
  24.6 2.4 scatter_custom_fusion
  27.1 12.2 %all-gather.2.cloned.1.call-done = bf16[128,4096]{1,0:T(8,128)(2,1)} async-done(((bf16[128,1024]{1,0:T(8,128)(2,1)}), bf16[128,4096]{1,0:T(8,128)(2,1)}) %all-gather.2.cloned.1.call-update) | async-done | bytes 1048592 | tf_op jit(solution)/shard_map/all_gather | solution.py:30
  39.2 16.4 %gather_fusion = bf16[1024,4096]{1,0:T(8,128)(2,1)} fusion(bf16[128,4096]{1,0:T(8,128)(2,1)} %all-gather.2.cloned.1.call-done, s32[1024]{0:T(1024)S(1)} %fusion.15), kind=kCustom, calls=%fused_computation | custom fusion | bytes 16781312 | tf_op jit(solution)/shard_map/gather | solution.py:31
  55.7 10.8 %all-to-all-start.1 = ((bf16[64,16,4096]{2,1,0:T(8,128)(2,1)}), bf16[64,16,4096]{2,1,0:T(8,128)(2,1)}, u32[]{:S(2)}, u32[]{:S(2)}) async-start(bf16[64,16,4096]{2,1,0:T(8,128)(2,1)} %bitcast.60), calls=%async_computation.1 | async-start | bytes 16777216 | tf_op jit(solution)/shard_map/all_to_all | solution.py:33
  66.7 1.2 convert_reduce_fusion.1
  68.0 182.8 %all-to-all-done.1 = bf16[64,16,4096]{2,1,0:T(8,128)(2,1)} async-done(((bf16[64,16,4096]{2,1,0:T(8,128)(2,1)}), bf16[64,16,4096]{2,1,0:T(8,128)(2,1)}, u32[]{:S(2)}, u32[]{:S(2)}) %all-to-all-start.1) | async-done | bytes 8388640 | tf_op jit(solution)/shard_map/all_to_all | solution.py:33
  250.8 7.2 %broadcast_select_fusion = bf16[64,16,4096]{2,1,0:T(8,128)(2,1)} fusion(bf16[64,16,4096]{2,1,0:T(8,128)(2,1)} %all-to-all-done.1, pred[64,16]{1,0:T(8,128)(4,1)S(1)} %iota_compare_fusion.5), kind=kLoop, calls=%fused_computation.3 | loop fusion | flops 4194304 | bytes 16778240 | tf_op jit(solution)/shard_map/jit(_where)/select_n | solution.py:39
  258.0 8.0 %fusion.3 = f32[1024,384]{1,0:T(8,128)S(1)} fusion(bf16[1024,4096]{1,0:T(8,128)(2,1)} %bitcast.61, bf16[1,4096,384]{2,1,0:T(8,128)(2,1)} %param.10), kind=kOutput, calls=%fused_computation.8 | convolution fusion | flops 3221225472 | bytes 13107200 | tf_op jit(solution)/shard_map/dot_general | solution.py:45
  266.0 4.6 multiply_convert_fusion
  271.5 6.6 %convolution_convert_fusion = bf16[64,16,4096]{2,1,0:T(8,128)(2,1)} fusion(bf16[64,16,384]{2,1,0:T(8,128)(2,1)S(1)} %bitcast.63, bf16[1,384,4096]{2,1,0:T(8,128)(2,1)S(1)} %copy-done), kind=kOutput, calls=%fused_computation.4 | convolution fusion | flops 3225419776 | bytes 12320768 | tf_op jit(solution)/shard_map/dot_general | solution.py:48
  278.2 80.3 %reduce-scatter.2.cloned.1.call-done = bf16[64,16,1024]{2,1,0:T(8,128)(2,1)} async-done(((bf16[64,16,4096]{2,1,0:T(8,128)(2,1)}), bf16[64,16,1024]{2,1,0:T(8,128)(2,1)}) %reduce-scatter.2.cloned.1.call-update) | async-done | bytes 2097168 | tf_op jit(solution)/shard_map/reduce_scatter | solution.py:49
  358.5 10.8 %all-to-all-start.2 = ((bf16[64,16,1024]{2,1,0:T(8,128)(2,1)}), bf16[64,16,1024]{2,1,0:T(8,128)(2,1)}, u32[]{:S(2)}, u32[]{:S(2)}) async-start(bf16[64,16,1024]{2,1,0:T(8,128)(2,1)} %reduce-scatter.2.cloned.1.call-done), calls=%async_computation.3 | async-start | bytes 4194304 | tf_op jit(solution)/shard_map/all_to_all | solution.py:55
  369.5 2.2 convolution_convert_fusion.1
  371.9 47.3 %all-reduce.2.cloned.1.call-done = bf16[1024,128]{1,0:T(8,128)(2,1)} async-done(((bf16[1024,128]{1,0:T(8,128)(2,1)}), bf16[1024,128]{1,0:T(8,128)(2,1)}) %all-reduce.2.cloned.1.call-update) | async-done | bytes 262160 | tf_op jit(solution)/shard_map/psum | solution.py:66
  419.2 1.3 fusion.20
  420.7 11.7 %cholesky.17 = f32[128,128]{1,0:T(8,128)S(1)} custom-call(f32[128,128]{1,0:T(8,128)S(1)} %fusion.13), custom_call_target="Cholesky" | custom-call | tf_op jit(solution)/shard_map/jit(cholesky)/cholesky | solution.py:67
  433.7 9.8 %custom-call.7 = f32[1,128,128]{1,2,0:T(8,128)S(1)} custom-call(f32[1,128,128]{2,1,0:T(8,128)S(1)} %fusion.10), custom_call_target="InvertDiagBlocksLowerTriangular" | custom-call | tf_op jit(solution)/shard_map/jit(_solve_triangular)/triangular_solve | solution.py:71
  443.5 1.5 fusion.21
  445.1 1.0 convolution_bitcast_fusion
  446.1 5.3 %gather_fusion.1 = bf16[512,1024]{1,0:T(8,128)(2,1)} fusion(bf16[1024,1024]{1,0:T(8,128)(2,1)} %bitcast.11, s32[1024]{0:T(1024)S(1)} %pad_clamp_fusion), kind=kCustom, calls=%fused_computation.1 | custom fusion | bytes 2099200 | tf_op jit(solution)/shard_map/gather | solution.py:56
  451.5 2.3 reshape.115
  453.7 1.9 fusion.19
  (45 shorter events, 8.0 us)
Async XLA Ops:
  7.2 264.3 %copy-start = (bf16[1,384,4096]{2,1,0:T(8,128)(2,1)S(1)}, bf16[1,384,4096]{2,1,0:T(8,128)(2,1)}, u32[]{:S(2)}) copy-start(bf16[1,384,4096]{2,1,0:T(8,128)(2,1)} %param.12) | copy-start | bytes 9437188
  7.2 32.0 %all-gather.2.cloned.1.call-start = ((), (), s32[]{:S(2)}) async-start(), calls=%async_computation.4 | async-start | bytes 1310720 | tf_op jit(solution)/shard_map/all_gather | solution.py:30
  11.5 44.1 %all-to-all-start = ((bf16[64,1,1]{2,1,0:T(2,128)(2,1)}), bf16[64,1,1]{2,1,0:T(2,128)(2,1)S(1)}, u32[]{:S(2)}, u32[]{:S(2)}) async-start(bf16[64,1,1]{2,1,0:T(2,128)(2,1)} %copy.22), calls=%async_computation | async-start | bytes 65536 | tf_op jit(solution)/shard_map/all_to_all | solution.py:34
  55.7 195.1 %all-to-all-start.1 = ((bf16[64,16,4096]{2,1,0:T(8,128)(2,1)}), bf16[64,16,4096]{2,1,0:T(8,128)(2,1)}, u32[]{:S(2)}, u32[]{:S(2)}) async-start(bf16[64,16,4096]{2,1,0:T(8,128)(2,1)} %bitcast.60), calls=%async_computation.1 | async-start | bytes 16777216 | tf_op jit(solution)/shard_map/all_to_all | solution.py:33
  66.4 292.0 %reduce-scatter.2.cloned.1.call-start = ((), (), s32[]{:S(2)}) async-start(), calls=%async_computation.5 | async-start | bytes 10485760 | tf_op jit(solution)/shard_map/reduce_scatter | solution.py:49
  258.0 8.0 %copy-start.1 = (bf16[64,16,4096]{2,1,0:T(8,128)(2,1)S(1)}, bf16[64,16,4096]{2,1,0:T(8,128)(2,1)}, u32[]{:S(2)}) copy-start(bf16[64,16,4096]{2,1,0:T(8,128)(2,1)} %broadcast_select_fusion) | copy-start | bytes 25165828
  258.0 8.0 %copy-start.5 = (bf16[1,4096,384]{2,1,0:T(8,128)(2,1)S(1)}, bf16[1,4096,384]{2,1,0:T(8,128)(2,1)}, u32[]{:S(2)}) copy-start(bf16[1,4096,384]{2,1,0:T(8,128)(2,1)} %param.11) | copy-start | bytes 9437188
  270.6 0.9 copy-start.2
  278.1 91.4 %copy-start.3 = (bf16[384,128]{1,0:T(8,128)(2,1)S(1)}, bf16[384,128]{1,0:T(8,128)(2,1)}, u32[]{:S(2)}) copy-start(bf16[384,128]{1,0:T(8,128)(2,1)} %param.13) | copy-start | bytes 294916
  278.2 93.6 %copy-start.4 = (f32[128,4]{0,1:T(4,128)S(1)}, f32[128,4]{0,1:T(4,128)}, u32[]{:S(2)}) copy-start(f32[128,4]{0,1:T(4,128)} %param.9) | copy-start | bytes 6148
  358.5 87.7 %all-to-all-start.2 = ((bf16[64,16,1024]{2,1,0:T(8,128)(2,1)}), bf16[64,16,1024]{2,1,0:T(8,128)(2,1)}, u32[]{:S(2)}, u32[]{:S(2)}) async-start(bf16[64,16,1024]{2,1,0:T(8,128)(2,1)} %reduce-scatter.2.cloned.1.call-done), calls=%async_computation.3 | async-start | bytes 4194304 | tf_op jit(solution)/shard_map/all_to_all | solution.py:55
  369.2 50.0 %all-reduce.2.cloned.1.call-start = ((), (), s32[]{:S(2)}) async-start(), calls=%async_computation.6 | async-start | bytes 524288 | tf_op jit(solution)/shard_map/psum | solution.py:66
Sparse Core Ops, SparseCore 0:
  9.8 29.3 all-gather.1
  278.3 80.1 reduce-scatter.1
  373.0 46.2 all-reduce.1
where the time goes:
time: 464 us; the launch traced here: 463 us
  waiting for transfers between devices  323 us (70%)
  starting transfers between devices  34.1 us (7%)
  other arithmetic  33.6 us (7%)
  local copies, waits for them, and re-layouts  30.8 us (7%)
  matrix products  27.2 us (6%)
  between operations  14 us (3%)
    all_to_all x1, waiting for transfers between devices, body(): lax.all_to_all(outgoing, 'expert', split_axis=0, concat_axis=0, tiled=True)  183 us
    reduce_scatter x1, waiting for transfers between devices, body(): lax.psum_scatter(partial_value.reshape(owners, capacity, width).astype(jn...  80.3 us
    psum x1, waiting for transfers between devices, body(): lax.psum(sketch_part.astype(jnp.bfloat16), 'dp').astype(jnp.float32)  47.3 us
    gather x1, local copies, waits for them, and re-layouts, body(): features[source_token].reshape(owners, capacity, features.shape[1])  16.4 us
    another operation x3, other arithmetic, body(): jnp.linalg.cholesky(gram_matrix(sketch_full) + ridge_term * eye_matrix)  12.4 us
    all_gather x1, waiting for transfers between devices, body(): features = lax.all_gather(tokens, 'dp', axis=1, tiled=True)  12.2 us
    all_to_all x1, starting transfers between devices, body(): lax.all_to_all(count_wire, 'expert', split_axis=0, concat_axis=0, tiled=T...  12.1 us
    all_to_all x1, starting transfers between devices, body(): lax.all_to_all(sums, 'expert', split_axis=0, concat_axis=0, tiled=True)  10.8 us
  transfers between devices with their start and end apart: 6, of which 4 were waited for; matrix products, arithmetic and copies ran while one was open for 12% of the time, Pallas kernels for 0%

commit v1 on v0

--- a/solution.py
+++ b/solution.py
@@ -4,6 +4,19 @@
 from jax.sharding import PartitionSpec as P
 
 ridge_term = 1.0
+
+
+def ring_gather(x, axis, dim):
+    ways = lax.axis_size(axis)
+    up = [(d, (d + 1) % ways) for d in range(ways)]
+    down = [(d, (d - 1) % ways) for d in range(ways)]
+    earlier, later = ([x], [x])
+    for _ in range(ways // 2):
+        earlier.append(lax.ppermute(earlier[-1], axis, up))
+    for _ in range((ways - 1) // 2):
+        later.append(lax.ppermute(later[-1], axis, down))
+    line = jnp.concatenate([*earlier[::-1], *later[1:]], axis=dim)
+    return jnp.roll(line, (lax.axis_index(axis) - ways // 2) * x.shape[dim], axis=dim)
 
 
 def gram_matrix(factor_rows):
@@ -27,7 +40,7 @@
     )
     source_token = source_pair // route_count
     count_wire = counts.astype(jnp.bfloat16)
-    features = lax.all_gather(tokens, "dp", axis=1, tiled=True)
+    features = ring_gather(tokens, "dp", 1)
     outgoing = features[source_token].reshape(owners, capacity, features.shape[1])
     arrived, arrived_counts = (
         lax.all_to_all(outgoing, "expert", split_axis=0, concat_axis=0, tiled=True),

time: 464 us -> 469 us (1.011)
  waiting for transfers between devices: 323 us -> 316 us
  local copies, waits for them, and re-layouts: 30.8 us -> 37.6 us
    all_gather x1 -> x0, waiting for transfers between devices: 12.2 us -> none  [body(): features = lax.all_gather(tokens, 'dp', axis=1, tiled=True)]
    ppermute x0 -> x3, waiting for transfers between devices: none -> 7.13 us  [the longest x2 7.12 us: ring_gather(): earlier.append(lax.ppermute(earlier[-1], axis, up))]
  transfers between devices with their start and end apart: 6 -> 8, of which waited for: 4 -> 4; matrix products, arithmetic and copies ran while one was open for 12% -> 13% of each run, Pallas kernels for 0% -> 0%
where the time goes in v1:
time: 469 us; the launch traced here: 468 us
  waiting for transfers between devices  316 us (67%)
  local copies, waits for them, and re-layouts  37.6 us (8%)
  starting transfers between devices  37.5 us (8%)
  other arithmetic  35.4 us (8%)
  matrix products  27.2 us (6%)
  between operations  14.3 us (3%)
    all_to_all x1, waiting for transfers between devices, body(): lax.all_to_all(outgoing, 'expert', split_axis=0, concat_axis=0, tiled=True)  183 us
    reduce_scatter x1, waiting for transfers between devices, body(): lax.psum_scatter(partial_value.reshape(owners, capacity, width).astype(jn...  78.8 us
    psum x1, waiting for transfers between devices, body(): lax.psum(sketch_part.astype(jnp.bfloat16), 'dp').astype(jnp.float32)  47.4 us
    gather x1, local copies, waits for them, and re-layouts, body(): features[source_token].reshape(owners, capacity, features.shape[1])  16.4 us
    another operation x3, other arithmetic, body(): jnp.linalg.cholesky(gram_matrix(sketch_full) + ridge_term * eye_matrix)  12.4 us
    all_to_all x1, starting transfers between devices, body(): lax.all_to_all(count_wire, 'expert', split_axis=0, concat_axis=0, tiled=T...  12.1 us
    all_to_all x1, starting transfers between devices, body(): lax.all_to_all(sums, 'expert', split_axis=0, concat_axis=0, tiled=True)  10.8 us
    all_to_all x1, starting transfers between devices, body(): lax.all_to_all(outgoing, 'expert', split_axis=0, concat_axis=0, tiled=True)  10.5 us
  transfers between devices with their start and end apart: 8, of which 4 were waited for; matrix products, arithmetic and copies ran while one was open for 13% of the time, Pallas kernels for 0%

profile of v1, /device:TPU:8, one launch (start us, length us, event | category | flops | bytes accessed | tf_op | source)
XLA Modules:
  0.0 468.1 jit_solution(14223786993040600681)
XLA Ops:
  7.2 1.6 collective-permute-start
  8.8 1.7 collective-permute-start.2
  12.2 2.4 reduce-window.6
  15.8 12.1 %all-to-all-start = ((bf16[64,1,1]{2,1,0:T(2,128)(2,1)}), bf16[64,1,1]{2,1,0:T(2,128)(2,1)S(1)}, u32[]{:S(2)}, u32[]{:S(2)}) async-start(bf16[64,1,1]{2,1,0:T(2,128)(2,1)} %copy.22), calls=%async_computation | async-start | bytes 65536 | tf_op jit(solution)/shard_map/all_to_all | solution.py:47
  29.2 2.4 scatter_custom_fusion
  31.6 7.1 %collective-permute-done.1 = bf16[128,1024]{1,0:T(8,128)(2,1)} collective-permute-done((bf16[128,1024]{1,0:T(8,128)(2,1)}, bf16[128,1024]{1,0:T(8,128)(2,1)}, u32[]{:S(2)}, u32[]{:S(2)}) %collective-permute-start.1) | collective-permute-done | bytes 262176 | tf_op jit(solution)/shard_map/ppermute | solution.py:15
  45.7 16.4 %gather_fusion = bf16[1024,4096]{1,0:T(8,128)(2,1)} fusion(bf16[128,4096]{1,0:T(8,128)(2,1)} %constant_dynamic-slice_fusion, s32[1024]{0:T(1024)S(1)} %fusion.15), kind=kCustom, calls=%fused_computation | custom fusion | bytes 16781312 | tf_op jit(solution)/shard_map/gather | solution.py:44
  62.2 10.5 %all-to-all-start.1 = ((bf16[64,16,4096]{2,1,0:T(8,128)(2,1)}), bf16[64,16,4096]{2,1,0:T(8,128)(2,1)}, u32[]{:S(2)}, u32[]{:S(2)}) async-start(bf16[64,16,4096]{2,1,0:T(8,128)(2,1)} %bitcast.60), calls=%async_computation.1 | async-start | bytes 16777216 | tf_op jit(solution)/shard_map/all_to_all | solution.py:46
  74.2 182.8 %all-to-all-done.1 = bf16[64,16,4096]{2,1,0:T(8,128)(2,1)} async-done(((bf16[64,16,4096]{2,1,0:T(8,128)(2,1)}), bf16[64,16,4096]{2,1,0:T(8,128)(2,1)}, u32[]{:S(2)}, u32[]{:S(2)}) %all-to-all-start.1) | async-done | bytes 8388640 | tf_op jit(solution)/shard_map/all_to_all | solution.py:46
  257.1 7.2 %broadcast_select_fusion = bf16[64,16,4096]{2,1,0:T(8,128)(2,1)} fusion(bf16[64,16,4096]{2,1,0:T(8,128)(2,1)} %all-to-all-done.1, pred[64,16]{1,0:T(8,128)(4,1)S(1)} %iota_compare_fusion.5), kind=kLoop, calls=%fused_computation.3 | loop fusion | flops 4194304 | bytes 16778240 | tf_op jit(solution)/shard_map/jit(_where)/select_n | solution.py:52
  264.3 8.0 %fusion.3 = f32[1024,384]{1,0:T(8,128)S(1)} fusion(bf16[1024,4096]{1,0:T(8,128)(2,1)} %bitcast.61, bf16[1,4096,384]{2,1,0:T(8,128)(2,1)} %param.10), kind=kOutput, calls=%fused_computation.8 | convolution fusion | flops 3221225472 | bytes 13107200 | tf_op jit(solution)/shard_map/dot_general | solution.py:58
  272.3 4.6 multiply_convert_fusion
  277.7 6.6 %convolution_convert_fusion = bf16[64,16,4096]{2,1,0:T(8,128)(2,1)} fusion(bf16[64,16,384]{2,1,0:T(8,128)(2,1)S(1)} %bitcast.63, bf16[1,384,4096]{2,1,0:T(8,128)(2,1)S(1)} %copy-done), kind=kOutput, calls=%fused_computation.4 | convolution fusion | flops 3225419776 | bytes 12320768 | tf_op jit(solution)/shard_map/dot_general | solution.py:61
  284.4 78.8 %reduce-scatter.2.cloned.1.call-done = bf16[64,16,1024]{2,1,0:T(8,128)(2,1)} async-done(((bf16[64,16,4096]{2,1,0:T(8,128)(2,1)}), bf16[64,16,1024]{2,1,0:T(8,128)(2,1)}) %reduce-scatter.2.cloned.1.call-update) | async-done | bytes 2097168 | tf_op jit(solution)/shard_map/reduce_scatter | solution.py:62
  363.3 10.8 %all-to-all-start.2 = ((bf16[64,16,1024]{2,1,0:T(8,128)(2,1)}), bf16[64,16,1024]{2,1,0:T(8,128)(2,1)}, u32[]{:S(2)}, u32[]{:S(2)}) async-start(bf16[64,16,1024]{2,1,0:T(8,128)(2,1)} %reduce-scatter.2.cloned.1.call-done), calls=%async_computation.3 | async-start | bytes 4194304 | tf_op jit(solution)/shard_map/all_to_all | solution.py:68
  374.3 2.2 convolution_convert_fusion.1
  376.7 47.4 %all-reduce.2.cloned.1.call-done = bf16[1024,128]{1,0:T(8,128)(2,1)} async-done(((bf16[1024,128]{1,0:T(8,128)(2,1)}), bf16[1024,128]{1,0:T(8,128)(2,1)}) %all-reduce.2.cloned.1.call-update) | async-done | bytes 262160 | tf_op jit(solution)/shard_map/psum | solution.py:79
  424.1 1.3 fusion.20
  425.5 11.7 %cholesky.17 = f32[128,128]{1,0:T(8,128)S(1)} custom-call(f32[128,128]{1,0:T(8,128)S(1)} %fusion.13), custom_call_target="Cholesky" | custom-call | tf_op jit(solution)/shard_map/jit(cholesky)/cholesky | solution.py:80
  438.6 9.8 %custom-call.7 = f32[1,128,128]{1,2,0:T(8,128)S(1)} custom-call(f32[1,128,128]{2,1,0:T(8,128)S(1)} %fusion.10), custom_call_target="InvertDiagBlocksLowerTriangular" | custom-call | tf_op jit(solution)/shard_map/jit(_solve_triangular)/triangular_solve | solution.py:84
  448.4 1.5 fusion.21
  451.0 5.3 %gather_fusion.1 = bf16[512,1024]{1,0:T(8,128)(2,1)} fusion(bf16[1024,1024]{1,0:T(8,128)(2,1)} %bitcast.11, s32[1024]{0:T(1024)S(1)} %pad_clamp_fusion), kind=kCustom, calls=%fused_computation.1 | custom fusion | bytes 2099200 | tf_op jit(solution)/shard_map/gather | solution.py:69
  456.3 2.3 reshape.115
  458.6 1.9 fusion.19
  (59 shorter events, 17.2 us)
Async XLA Ops:
  7.2 270.6 %copy-start = (bf16[1,384,4096]{2,1,0:T(8,128)(2,1)S(1)}, bf16[1,384,4096]{2,1,0:T(8,128)(2,1)}, u32[]{:S(2)}) copy-start(bf16[1,384,4096]{2,1,0:T(8,128)(2,1)} %param.12) | copy-start | bytes 9437188
  7.2 33.5 %copy-start.3 = (bf16[128,1024]{1,0:T(8,128)(2,1)S(1)}, bf16[128,1024]{1,0:T(8,128)(2,1)}, u32[]{:S(2)}) copy-start(bf16[128,1024]{1,0:T(8,128)(2,1)} %param.7) | copy-start | bytes 786436
  7.2 21.6 %collective-permute-start = (bf16[128,1024]{1,0:T(8,128)(2,1)}, bf16[128,1024]{1,0:T(8,128)(2,1)}, u32[]{:S(2)}, u32[]{:S(2)}) collective-permute-start(bf16[128,1024]{1,0:T(8,128)(2,1)} %param.7), channel_id=1, source_target_pairs={{0,64},{64,128},{128,192},{192,0},{1,65},{65,129},{129,193},{193,1... | collective-permute-start | bytes 786440 | tf_op jit(solution)/shard_map/ppermute | solution.py:15
  8.8 32.0 %collective-permute-start.2 = (bf16[128,1024]{1,0:T(8,128)(2,1)}, bf16[128,1024]{1,0:T(8,128)(2,1)}, u32[]{:S(2)}, u32[]{:S(2)}) collective-permute-start(bf16[128,1024]{1,0:T(8,128)(2,1)} %param.7), channel_id=1, source_target_pairs={{0,192},{64,0},{128,64},{192,128},{1,193},{65,1},{129,65},{193,129... | collective-permute-start | bytes 786440 | tf_op jit(solution)/shard_map/ppermute | solution.py:17
  15.8 46.4 %all-to-all-start = ((bf16[64,1,1]{2,1,0:T(2,128)(2,1)}), bf16[64,1,1]{2,1,0:T(2,128)(2,1)S(1)}, u32[]{:S(2)}, u32[]{:S(2)}) async-start(bf16[64,1,1]{2,1,0:T(2,128)(2,1)} %copy.22), calls=%async_computation | async-start | bytes 65536 | tf_op jit(solution)/shard_map/all_to_all | solution.py:47
  28.8 10.0 %collective-permute-start.1 = (bf16[128,1024]{1,0:T(8,128)(2,1)}, bf16[128,1024]{1,0:T(8,128)(2,1)}, u32[]{:S(2)}, u32[]{:S(2)}) collective-permute-start(bf16[128,1024]{1,0:T(8,128)(2,1)} %collective-permute-done), channel_id=1, source_target_pairs={{0,64},{64,128},{128,192},{192,0},{1,65},{65,129},{129,193},{193,1... | collective-permute-start | bytes 786440 | tf_op jit(solution)/shard_map/ppermute | solution.py:15
  62.2 194.9 %all-to-all-start.1 = ((bf16[64,16,4096]{2,1,0:T(8,128)(2,1)}), bf16[64,16,4096]{2,1,0:T(8,128)(2,1)}, u32[]{:S(2)}, u32[]{:S(2)}) async-start(bf16[64,16,4096]{2,1,0:T(8,128)(2,1)} %bitcast.60), calls=%async_computation.1 | async-start | bytes 16777216 | tf_op jit(solution)/shard_map/all_to_all | solution.py:46
  72.7 290.6 %reduce-scatter.2.cloned.1.call-start = ((), (), s32[]{:S(2)}) async-start(), calls=%async_computation.4 | async-start | bytes 10485760 | tf_op jit(solution)/shard_map/reduce_scatter | solution.py:62
  264.3 8.0 %copy-start.1 = (bf16[64,16,4096]{2,1,0:T(8,128)(2,1)S(1)}, bf16[64,16,4096]{2,1,0:T(8,128)(2,1)}, u32[]{:S(2)}) copy-start(bf16[64,16,4096]{2,1,0:T(8,128)(2,1)} %broadcast_select_fusion) | copy-start | bytes 25165828
  264.3 8.0 %copy-start.6 = (bf16[1,4096,384]{2,1,0:T(8,128)(2,1)S(1)}, bf16[1,4096,384]{2,1,0:T(8,128)(2,1)}, u32[]{:S(2)}) copy-start(bf16[1,4096,384]{2,1,0:T(8,128)(2,1)} %param.11) | copy-start | bytes 9437188
  276.9 0.9 copy-start.2
  284.4 89.9 %copy-start.4 = (bf16[384,128]{1,0:T(8,128)(2,1)S(1)}, bf16[384,128]{1,0:T(8,128)(2,1)}, u32[]{:S(2)}) copy-start(bf16[384,128]{1,0:T(8,128)(2,1)} %param.13) | copy-start | bytes 294916
  284.4 92.1 %copy-start.5 = (f32[128,4]{0,1:T(4,128)S(1)}, f32[128,4]{0,1:T(4,128)}, u32[]{:S(2)}) copy-start(f32[128,4]{0,1:T(4,128)} %param.9) | copy-start | bytes 6148
  363.3 87.7 %all-to-all-start.2 = ((bf16[64,16,1024]{2,1,0:T(8,128)(2,1)}), bf16[64,16,1024]{2,1,0:T(8,128)(2,1)}, u32[]{:S(2)}, u32[]{:S(2)}) async-start(bf16[64,16,1024]{2,1,0:T(8,128)(2,1)} %reduce-scatter.2.cloned.1.call-done), calls=%async_computation.3 | async-start | bytes 4194304 | tf_op jit(solution)/shard_map/all_to_all | solution.py:68
  374.0 50.1 %all-reduce.2.cloned.1.call-start = ((), (), s32[]{:S(2)}) async-start(), calls=%async_computation.5 | async-start | bytes 524288 | tf_op jit(solution)/shard_map/psum | solution.py:79
Sparse Core Ops, SparseCore 0:
  284.5 78.6 reduce-scatter.1
  377.8 46.2 all-reduce.1
